TPU v7x, 512 devices: a whole 4x4x16 slice. The times are simulated.
512 devices in a mesh: grp: 8 (over x, core), path: 64 (over z, y).
Axes of the slice: x: 4, y: 4, z: 16, core: 2. Of those that a mesh axis runs over, the one named last changes fastest.
Arguments:
- normals: float32 [32, 8388608], P(None, ('grp', 'path')), may hold values from -10.1 to 10.1
- spot_today: float32 [32], replicated, may hold values from 0.5 to 2
- volatility: float32 [32], replicated, may hold values from 0.1 to 0.5
- weights: float32 [32], replicated, may hold values from 0.5 to 1.5
- cash_flows: float32 [8388608], P(('grp', 'path')), may hold values from -300 to 300
- exercise: int32 [8388608], P(('grp', 'path')), may hold values 0 or 1
Outputs:
- path_value: float32 [8388608], P(('grp', 'path'))
- state_cot: float32 [32, 8388608], P(None, ('grp', 'path'))
- flow_cot: float32 [8388608], P(('grp', 'path'))
- greeks: float32 [2, 32], replicated
All inputs are finite; a program needn't handle non-finite values. No bound on the sum of `exercise` on one device may be relied on, other than what follows from the above.
Results may differ from a plain program's by a relative error of at most 0.0003.
Values sent between devices are 32-bit elements; how exact they have to be, the bound alone decides.
A program may use at most 64 MiB of HBM per device.

v0:
```python
import math
import jax
import jax.numpy as jnp
from jax import lax
from jax.sharding import PartitionSpec as P

expiry_time = 0.5
root_time = math.sqrt(0.5)
inv_root_two = 1.0 / math.sqrt(2.0)
notional = 20.0
soft_width = 0.02


def path_state(normals, spot_today, volatility):
    return spot_today[:, None] * jnp.exp(
        volatility[:, None] * (root_time * normals) - 0.5 * expiry_time * volatility[:, None] ** 2
    )


def basis_rows(state, spot_today, volatility):
    scaled = (state / spot_today[:, None] - 1.0) / (volatility[:, None] * root_time)
    leading = jnp.ones_like(scaled[:1])
    squares = (scaled * scaled - 1.0) * inv_root_two
    neighbour = scaled * jnp.roll(scaled, -1, axis=0)
    bounded = jnp.tanh(scaled[:-1])
    return jnp.concatenate([leading, scaled, squares, neighbour, bounded], axis=0)


def payoff(state, spot_today, weights):
    basket = jnp.sum(weights[:, None] * state, axis=0) / jnp.sum(weights * spot_today)
    return notional * soft_width * jax.nn.softplus((basket - 1.0) / soft_width)


def chol_solve(factor, rhs):
    first = lax.linalg.triangular_solve(factor, rhs, left_side=True, lower=True)
    return lax.linalg.triangular_solve(factor, first, left_side=True, lower=True, transpose_a=True)


def per_device(normals, spot_today, volatility, weights, cash_flows, exercise):
    assets, local_paths = normals.shape
    features = 4 * assets
    block_width = math.gcd(local_paths, 1024)
    block_count = local_paths // block_width
    path_total = local_paths * lax.axis_size("grp") * lax.axis_size("path")
    highest = lax.Precision.HIGHEST
    contract_last = (((1,), (1,)), ((), ()))

    def block_inputs(block_index):
        block_start = block_index * block_width
        draw_block = lax.dynamic_slice_in_dim(normals, block_start, block_width, 1)
        flow_block = lax.dynamic_slice_in_dim(cash_flows, block_start, block_width, 0)
        taken_flag = lax.dynamic_slice_in_dim(exercise, block_start, block_width, 0).astype(
            jnp.float32
        )
        return (draw_block, flow_block, taken_flag)

    def gram_step(block_index, running):
        gram_acc, moment_acc = running
        draw_block, flow_block, taken_flag = block_inputs(block_index)
        basis_block = basis_rows(
            path_state(draw_block, spot_today, volatility), spot_today, volatility
        )
        gram_acc = gram_acc + lax.dot_general(
            basis_block,
            basis_block,
            contract_last,
            precision=highest,
            preferred_element_type=jnp.float32,
        )
        targets = jnp.stack([flow_block, 1.0 - taken_flag])
        moment_acc = moment_acc + lax.dot_general(
            targets,
            basis_block,
            contract_last,
            precision=highest,
            preferred_element_type=jnp.float32,
        )
        return (gram_acc, moment_acc)

    zero_gram = jnp.zeros((features, features), jnp.float32)
    zero_moment = jnp.zeros((2, features), jnp.float32)
    gram_acc, moment_acc = lax.fori_loop(0, block_count, gram_step, (zero_gram, zero_moment))
    gram_sum, moment_sum = lax.psum((gram_acc, moment_acc), ("grp", "path"))
    gram_mean = gram_sum / path_total
    moment_mean = moment_sum / path_total
    factor = jnp.linalg.cholesky(gram_mean)
    coefficients = chol_solve(factor, moment_mean.T)
    regression = coefficients[:, 0]
    multiplier = coefficients[:, 1]
    coef_rows = coefficients.T

    def adjoint_step(block_index, running):
        value_out, state_out, flow_out, greek_acc = running
        draw_block, flow_block, taken_flag = block_inputs(block_index)
        state, path_back = jax.vjp(
            lambda spot_level, spread: path_state(draw_block, spot_level, spread),
            spot_today,
            volatility,
        )
        (basis_block, reward), feature_back = jax.vjp(
            lambda current, spot_level, spread: (
                basis_rows(current, spot_level, spread),
                payoff(current, spot_level, weights),
            ),
            state,
            spot_today,
            volatility,
        )
        fitted = lax.dot_general(
            coef_rows,
            basis_block,
            (((1,), (0,)), ((), ())),
            precision=highest,
            preferred_element_type=jnp.float32,
        )
        continuation = fitted[0]
        lam_phi = fitted[1]
        value_block = taken_flag * reward + (1.0 - taken_flag) * continuation
        rows_bar = (
            multiplier[:, None] * (flow_block - continuation)[None, :]
            + regression[:, None] * (1.0 - taken_flag - lam_phi)[None, :]
        )
        state_bar, spot_bar, spread_bar = feature_back((rows_bar, taken_flag))
        spot_path, spread_path = path_back(state_bar)
        greek_acc = greek_acc + jnp.stack([spot_bar + spot_path, spread_bar + spread_path])
        block_start = block_index * block_width
        value_out = lax.dynamic_update_slice_in_dim(value_out, value_block, block_start, 0)
        state_out = lax.dynamic_update_slice_in_dim(state_out, state_bar, block_start, 1)
        flow_out = lax.dynamic_update_slice_in_dim(flow_out, lam_phi, block_start, 0)
        return (value_out, state_out, flow_out, greek_acc)

    start_outs = (
        jnp.zeros((local_paths,), jnp.float32),
        jnp.zeros((assets, local_paths), jnp.float32),
        jnp.zeros((local_paths,), jnp.float32),
        jnp.zeros((2, assets), jnp.float32),
    )
    path_value, state_cot, flow_cot, greek_acc = lax.fori_loop(
        0, block_count, adjoint_step, start_outs
    )
    greeks = lax.psum(greek_acc, ("grp", "path")) / path_total
    return (path_value, state_cot, flow_cot, greeks)


def solution(mesh):
    in_specs = (P(None, ("grp", "path")), P(), P(), P(), P(("grp", "path")), P(("grp", "path")))
    out_specs = (P(("grp", "path")), P(None, ("grp", "path")), P(("grp", "path")), P())
    return jax.shard_map(
        per_device, mesh=mesh, in_specs=in_specs, out_specs=out_specs, check_vma=False
    )
```

profile of v0, /device:TPU:1, one launch (start us, length us, event | category | flops | bytes accessed | tf_op | source)
XLA Modules:
  0.0 799.2 jit_solution(2905008628798093460)
XLA Ops:
  7.9 80.4 %while.42 = (s32[]{:T(128)}, f32[128,128]{1,0:T(8,128)S(1)}, f32[2,128]{1,0:T(2,128)S(1)}, f32[32]{0:T(128)}, f32[32,16384]{1,0:T(8,128)}, /*index=5*/f32[32]{0:...) while((s32[]{:T(128)}, f32[128,128]{1,0:T(8,128)S(1)}, ...), condition=%wide.region_1.2_spmd.clone, body=%wide.region_0.1_spmd.clone.sunk | while | flops 204870208 | bytes 3562582 | solution.py:82
  91.7 111.2 %psum.22 = f32[2,128]{1,0:T(2,128)S(1)} all-reduce(f32[2,128]{1,0:T(2,128)S(1)} %get-tuple-element.642), channel_id=1, replica_groups=mesh['grp'=8,'path'=64] {'grp','path'}, use_global_device_ids=true, to_apply=%region_5.6 | all-reduce | flops 256 | bytes 2048 | tf_op jit(solution)/shard_map/psum | solution.py:83
  202.9 340.4 %all-reduce.5.cloned.1.call-done = f32[128,128]{0,1:T(8,128)} async-done(((f32[128,128]{0,1:T(8,128)}), f32[128,128]{0,1:T(8,128)}) %all-reduce.5.cloned.1.call-update) | async-done | bytes 65552 | tf_op jit(solution)/shard_map/psum | solution.py:83
  545.1 11.7 %cholesky.15 = f32[128,128]{1,0:T(8,128)S(1)} custom-call(f32[128,128]{1,0:T(8,128)S(1)} %fusion.19), custom_call_target="Cholesky" | custom-call | tf_op jit(solution)/shard_map/jit(cholesky)/cholesky | solution.py:86
  558.1 9.8 %custom-call.8 = f32[1,128,128]{1,2,0:T(8,128)S(1)} custom-call(f32[1,128,128]{2,1,0:T(8,128)S(1)} %fusion.14), custom_call_target="InvertDiagBlocksLowerTriangular" | custom-call | tf_op jit(solution)/shard_map/triangular_solve | solution.py:36
  568.7 121.5 %while.43 = (s32[]{:T(128)}, f32[16384]{0:T(1024)S(1)}, f32[32,16384]{1,0:T(8,128)S(1)}, f32[16384]{0:T(1024)S(1)}, f32[2,32]{1,0:T(2,128)S(1)}, /*index=5*/s32[...) while((s32[]{:T(128)}, f32[16384]{0:T(1024)S(1)}, ...), condition=%wide.region_15.16_spmd.clone, body=%wide.region_7.15_spmd.clone.sunk | while | flops 5333607 | bytes 5730625 | solution.py:138
  571.3 2.0 multiply_reduce_fusion.8
  574.8 1.3 fusion.49
  578.9 2.0 multiply_reduce_fusion.8
  582.4 1.3 fusion.49
  586.5 2.0 multiply_reduce_fusion.8
  590.0 1.3 fusion.49
  594.1 2.0 multiply_reduce_fusion.8
  597.6 1.3 fusion.49
  601.7 2.0 multiply_reduce_fusion.8
  605.2 1.3 fusion.49
  609.3 2.0 multiply_reduce_fusion.8
  616.9 2.0 multiply_reduce_fusion.8
  620.4 1.3 fusion.49
  624.5 2.0 multiply_reduce_fusion.8
  632.1 2.0 multiply_reduce_fusion.8
  635.6 1.3 fusion.49
  639.7 2.0 multiply_reduce_fusion.8
  647.3 2.0 multiply_reduce_fusion.8
  654.9 2.0 multiply_reduce_fusion.8
  658.4 1.3 fusion.49
  662.5 2.0 multiply_reduce_fusion.8
  670.1 2.0 multiply_reduce_fusion.8
  673.6 1.3 fusion.49
  677.7 2.0 multiply_reduce_fusion.8
  685.2 2.0 multiply_reduce_fusion.8
  690.3 101.5 %psum.23 = f32[2,32]{1,0:T(2,128)S(1)} all-reduce(f32[2,32]{1,0:T(2,128)S(1)} %get-tuple-element.646), channel_id=1, replica_groups=mesh['grp'=8,'path'=64] {'grp','path'}, use_global_device_ids=true, to_apply=%region_16.17 | all-reduce | flops 64 | bytes 512 | tf_op jit(solution)/shard_map/psum | solution.py:141
  (552 shorter events, 150.8 us)
Async XLA Ops:
  7.2 536.1 %all-reduce.5.cloned.1.call-start = ((), (), s32[]{:S(2)}) async-start(), calls=%async_computation | async-start | bytes 131072 | tf_op jit(solution)/shard_map/psum | solution.py:83
  7.9 81.2 %copy-start.1 = (f32[32]{0:T(128)S(1)}, f32[32]{0:T(128)}, u32[]{:S(2)}) copy-start(f32[32]{0:T(128)} %param.13) | copy-start | bytes 388
  88.3 480.4 %copy-start.2 = (f32[32]{0:T(128)S(1)}, f32[32]{0:T(128)}, u32[]{:S(2)}) copy-start(f32[32]{0:T(128)} %get-tuple-element.1153) | copy-start | bytes 388
  88.3 480.4 %copy-start.5 = (f32[32]{0:T(128)S(1)}, f32[32]{0:T(128)}, u32[]{:S(2)}) copy-start(f32[32]{0:T(128)} %get-tuple-element.1154) | copy-start | bytes 388
  690.2 102.1 %copy-start = (f32[32,16384]{1,0:T(8,128)}, f32[32,16384]{1,0:T(8,128)S(1)}, u32[]{:S(2)}) copy-start(f32[32,16384]{1,0:T(8,128)S(1)} %get-tuple-element.638) | copy-start | bytes 6291460
  690.3 102.1 %copy-start.3 = (f32[16384]{0:T(1024)}, f32[16384]{0:T(1024)S(1)}, u32[]{:S(2)}) copy-start(f32[16384]{0:T(1024)S(1)} %get-tuple-element.639) | copy-start | bytes 196612
  690.3 102.1 %copy-start.4 = (f32[16384]{0:T(1024)}, f32[16384]{0:T(1024)S(1)}, u32[]{:S(2)}) copy-start(f32[16384]{0:T(1024)S(1)} %get-tuple-element.637) | copy-start | bytes 196612
Sparse Core Ops, SparseCore 0:
  89.2 454.0 all-reduce.4
where the time goes:
time: 803 us; the launch traced here: 799 us
  waiting for transfers between devices  340 us (42%)
  blocking collectives  213 us (27%)
  other arithmetic  151 us (19%)
  local copies, waits for them, and re-layouts  40.1 us (5%)
  matrix products  24.6 us (3%)
  between operations  15.5 us (2%)
  loops' own time  14.4 us (2%)
    psum x1, waiting for transfers between devices, per_device(): gram_sum, moment_sum = lax.psum((gram_acc, moment_acc), ('grp', 'path'))  340 us
    psum x1, blocking collectives, per_device(): gram_sum, moment_sum = lax.psum((gram_acc, moment_acc), ('grp', 'path'))  111 us
    psum x1, blocking collectives, per_device(): greeks = lax.psum(greek_acc, ('grp', 'path')) / path_total  101 us
    mul x32, other arithmetic, basis_rows(): squares = (scaled * scaled - 1.0) * inv_root_two  33.1 us
    reduce_sum x16, other arithmetic, payoff(): jnp.sum(weights[:, None] * state, axis=0) / jnp.sum(weights * spot_today)  31.9 us
    concatenate x32, local copies, waits for them, and re-layouts, basis_rows(): jnp.concatenate([leading, scaled, squares, neighbour, bounded], axis=0)  21.9 us
    reduce_sum x16, other arithmetic, path_state(): volatility[:, None] * (root_time * normals)  21.4 us
  transfers between devices with their start and end apart: 1, of which 1 were waited for; matrix products, arithmetic and copies ran while one was open for 0% of the time, Pallas kernels for 0%

commit v1 on v0

--- a/solution.py
+++ b/solution.py
@@ -9,6 +9,12 @@
 inv_root_two = 1.0 / math.sqrt(2.0)
 notional = 20.0
 soft_width = 0.02
+
+
+def edit_files(work_x):
+    carry_in = lax.psum(work_x, "path")
+    main = lax.psum(carry_in, "grp")
+    return main
 
 
 def path_state(normals, spot_today, volatility):
@@ -80,7 +86,7 @@
     zero_gram = jnp.zeros((features, features), jnp.float32)
     zero_moment = jnp.zeros((2, features), jnp.float32)
     gram_acc, moment_acc = lax.fori_loop(0, block_count, gram_step, (zero_gram, zero_moment))
-    gram_sum, moment_sum = lax.psum((gram_acc, moment_acc), ("grp", "path"))
+    gram_sum, moment_sum = edit_files((gram_acc, moment_acc))
     gram_mean = gram_sum / path_total
     moment_mean = moment_sum / path_total
     factor = jnp.linalg.cholesky(gram_mean)

time: 803 us -> 769 us (0.958)
  waiting for transfers between devices: 340 us -> 257 us
  blocking collectives: 213 us -> 263 us
    psum x1 -> x2, waiting for transfers between devices: 340 us -> 257 us  [the longest x1 257 us: edit_files(): carry_in = lax.psum(work_x, 'path')]
    psum x1 -> x2, blocking collectives: 111 us -> 165 us  [the longest x1 113 us: edit_files(): carry_in = lax.psum(work_x, 'path')]
  transfers between devices with their start and end apart: 1 -> 2, of which waited for: 1 -> 1; matrix products, arithmetic and copies ran while one was open for 0% -> 0% of each run, Pallas kernels for 0% -> 0%
where the time goes in v1:
time: 769 us; the launch traced here: 766 us
  blocking collectives  263 us (34%)
  waiting for transfers between devices  257 us (33%)
  other arithmetic  151 us (20%)
  local copies, waits for them, and re-layouts  40.1 us (5%)
  matrix products  24.6 us (3%)
  between operations  15.5 us (2%)
  loops' own time  14.4 us (2%)
    psum x1, waiting for transfers between devices, edit_files(): carry_in = lax.psum(work_x, 'path')  257 us
    psum x1, blocking collectives, edit_files(): carry_in = lax.psum(work_x, 'path')  113 us
    psum x1, blocking collectives, per_device(): greeks = lax.psum(greek_acc, ('grp', 'path')) / path_total  98.7 us
    psum x1, blocking collectives, edit_files(): main = lax.psum(carry_in, 'grp')  51.3 us
    mul x32, other arithmetic, basis_rows(): squares = (scaled * scaled - 1.0) * inv_root_two  33.1 us
    reduce_sum x16, other arithmetic, payoff(): jnp.sum(weights[:, None] * state, axis=0) / jnp.sum(weights * spot_today)  31.9 us
    concatenate x32, local copies, waits for them, and re-layouts, basis_rows(): jnp.concatenate([leading, scaled, squares, neighbour, bounded], axis=0)  21.9 us
    reduce_sum x16, other arithmetic, path_state(): volatility[:, None] * (root_time * normals)  21.4 us
  transfers between devices with their start and end apart: 2, of which 1 were waited for; matrix products, arithmetic and copies ran while one was open for 0% of the time, Pallas kernels for 0%

profile of v1, /device:TPU:1, one launch (start us, length us, event | category | flops | bytes accessed | tf_op | source)
XLA Modules:
  0.0 766.0 jit_solution(15858422025448748077)
XLA Ops:
  7.9 80.4 %while.42 = (s32[]{:T(128)}, f32[128,128]{1,0:T(8,128)S(1)}, f32[2,128]{1,0:T(2,128)S(1)}, f32[32]{0:T(128)}, f32[32,16384]{1,0:T(8,128)}, /*index=5*/f32[32]{0:...) while((s32[]{:T(128)}, f32[128,128]{1,0:T(8,128)S(1)}, ...), condition=%wide.region_1.2_spmd.clone, body=%wide.region_0.1_spmd.clone.sunk | while | flops 204870208 | bytes 3562582 | solution.py:88
  89.1 256.7 %all-reduce.6.cloned.1.call-done = f32[128,128]{0,1:T(8,128)} async-done(((f32[128,128]{0,1:T(8,128)}), f32[128,128]{0,1:T(8,128)}) %all-reduce.6.cloned.1.call-update) | async-done | bytes 65552 | tf_op jit(solution)/shard_map/psum | solution.py:15
  348.5 113.2 %psum.37 = f32[2,128]{1,0:T(2,128)S(1)} all-reduce(f32[2,128]{1,0:T(2,128)S(1)} %get-tuple-element.642), channel_id=1, replica_groups=mesh['grp'=8,'path'=64] {'path'}, use_global_device_ids=true, to_apply=%region_6.7 | all-reduce | flops 256 | bytes 2048 | tf_op jit(solution)/shard_map/psum | solution.py:15
  461.7 51.3 %psum.38 = f32[2,128]{1,0:T(2,128)S(1)} all-reduce(f32[2,128]{1,0:T(2,128)S(1)} %psum.37), channel_id=1, replica_groups=mesh['grp'=8,'path'=64] {'grp'}, use_global_device_ids=true, to_apply=%region_7.8 | all-reduce | flops 256 | bytes 2048 | tf_op jit(solution)/shard_map/psum | solution.py:16
  514.8 11.7 %cholesky.15 = f32[128,128]{1,0:T(8,128)S(1)} custom-call(f32[128,128]{1,0:T(8,128)S(1)} %fusion.19), custom_call_target="Cholesky" | custom-call | tf_op jit(solution)/shard_map/jit(cholesky)/cholesky | solution.py:92
  527.8 9.8 %custom-call.8 = f32[1,128,128]{1,2,0:T(8,128)S(1)} custom-call(f32[1,128,128]{2,1,0:T(8,128)S(1)} %fusion.14), custom_call_target="InvertDiagBlocksLowerTriangular" | custom-call | tf_op jit(solution)/shard_map/triangular_solve | solution.py:42
  538.4 121.5 %while.43 = (s32[]{:T(128)}, f32[16384]{0:T(1024)S(1)}, f32[32,16384]{1,0:T(8,128)S(1)}, f32[16384]{0:T(1024)S(1)}, f32[2,32]{1,0:T(2,128)S(1)}, /*index=5*/s32[...) while((s32[]{:T(128)}, f32[16384]{0:T(1024)S(1)}, ...), condition=%wide.region_17.18_spmd.clone, body=%wide.region_9.17_spmd.clone.sunk | while | flops 5333607 | bytes 5730625 | solution.py:144
  541.0 2.0 multiply_reduce_fusion.8
  544.5 1.3 fusion.49
  548.6 2.0 multiply_reduce_fusion.8
  552.1 1.3 fusion.49
  556.2 2.0 multiply_reduce_fusion.8
  559.7 1.3 fusion.49
  563.8 2.0 multiply_reduce_fusion.8
  567.3 1.3 fusion.49
  571.4 2.0 multiply_reduce_fusion.8
  574.9 1.3 fusion.49
  579.0 2.0 multiply_reduce_fusion.8
  586.6 2.0 multiply_reduce_fusion.8
  594.2 2.0 multiply_reduce_fusion.8
  597.7 1.3 fusion.49
  601.8 2.0 multiply_reduce_fusion.8
  609.4 2.0 multiply_reduce_fusion.8
  612.9 1.3 fusion.49
  617.0 2.0 multiply_reduce_fusion.8
  624.6 2.0 multiply_reduce_fusion.8
  632.1 2.0 multiply_reduce_fusion.8
  639.7 2.0 multiply_reduce_fusion.8
  647.3 2.0 multiply_reduce_fusion.8
  650.9 1.3 fusion.49
  654.9 2.0 multiply_reduce_fusion.8
  660.0 98.7 %psum.39 = f32[2,32]{1,0:T(2,128)S(1)} all-reduce(f32[2,32]{1,0:T(2,128)S(1)} %get-tuple-element.646), channel_id=1, replica_groups=mesh['grp'=8,'path'=64] {'grp','path'}, use_global_device_ids=true, to_apply=%region_18.19 | all-reduce | flops 64 | bytes 512 | tf_op jit(solution)/shard_map/psum | solution.py:147
  (556 shorter events, 152.2 us)
Async XLA Ops:
  7.2 338.7 %all-reduce.6.cloned.1.call-start = ((), (), s32[]{:S(2)}) async-start(), calls=%async_computation | async-start | bytes 131072 | tf_op jit(solution)/shard_map/psum | solution.py:15
  7.9 338.0 %copy-start.1 = (f32[32]{0:T(128)S(1)}, f32[32]{0:T(128)}, u32[]{:S(2)}) copy-start(f32[32]{0:T(128)} %param.13) | copy-start | bytes 388
  88.3 450.1 %copy-start.2 = (f32[32]{0:T(128)S(1)}, f32[32]{0:T(128)}, u32[]{:S(2)}) copy-start(f32[32]{0:T(128)} %get-tuple-element.1154) | copy-start | bytes 388
  88.3 450.1 %copy-start.5 = (f32[32]{0:T(128)S(1)}, f32[32]{0:T(128)}, u32[]{:S(2)}) copy-start(f32[32]{0:T(128)} %get-tuple-element.1158) | copy-start | bytes 388
  89.1 423.9 %all-reduce.8.cloned.1.call-start = ((), (), s32[]{:S(2)}) async-start(), calls=%async_computation.1 | async-start | bytes 131072 | tf_op jit(solution)/shard_map/psum | solution.py:16
  659.9 99.3 %copy-start = (f32[32,16384]{1,0:T(8,128)}, f32[32,16384]{1,0:T(8,128)S(1)}, u32[]{:S(2)}) copy-start(f32[32,16384]{1,0:T(8,128)S(1)} %get-tuple-element.638) | copy-start | bytes 6291460
  659.9 99.2 %copy-start.3 = (f32[16384]{0:T(1024)}, f32[16384]{0:T(1024)S(1)}, u32[]{:S(2)}) copy-start(f32[16384]{0:T(1024)S(1)} %get-tuple-element.639) | copy-start | bytes 196612
  659.9 99.2 %copy-start.4 = (f32[16384]{0:T(1024)}, f32[16384]{0:T(1024)S(1)}, u32[]{:S(2)}) copy-start(f32[16384]{0:T(1024)S(1)} %get-tuple-element.637) | copy-start | bytes 196612
Sparse Core Ops, SparseCore 0:
  89.2 256.5 all-reduce.5
  348.1 78.6 all-reduce.7
